TPU v7x, 128 devices: a whole 4x4x4 slice. The times are simulated.
128 devices in a mesh: dp: 4 (over x), fy: 4 (over z_hi, core), fx: 8 (over z_lo, y).
Axes of the slice: x: 4, y: 4, z: 4 (z_hi: 2, z_lo: 2; z = z_hi * 2 + z_lo), core: 2. Of those that a mesh axis runs over, the one named last changes fastest.
Arguments:
- fine_tokens: bfloat16 [4, 64, 256, 768], P('dp', 'fy', 'fx'), may hold values from -40 to 40
- parent: int32 [4, 64, 64], P('dp', 'fy', 'fx'), may hold values from 0 to 511, as said below
- coarse_tokens: bfloat16 [4, 512, 768], P('dp', 'fx'), may hold values from -6 to 6
- tile_level: int32 [4, 512], P('dp', 'fx'), may hold values from 0 to 2
- level_table: float32 [3, 768], replicated, may hold values from -3 to 3
- norm_gain: float32 [768], replicated, may hold values from 0.5 to 1.5
- qkv_weight: bfloat16 [768, 2304], replicated, may hold values from -7 to 7
- out_weight: bfloat16 [768, 768], replicated, may hold values from -0.21875 to 0.21875
- cotangent: bfloat16 [4, 64, 256, 768], P('dp', 'fy', 'fx'), may hold values from -6 to 6
Outputs:
- mixed: bfloat16 [4, 64, 256, 768], P('dp', 'fy', 'fx')
- grad_tokens: bfloat16 [4, 64, 256, 768], P('dp', 'fy', 'fx')
- grad_coarse: float32 [4, 512, 768], P('dp', 'fx')
- grad_qkv: float32 [768, 2304], P('dp')
- grad_out: float32 [768, 768], P('dp')
- grad_gain: float32 [768], P('dp')
- grad_level: float32 [3, 768], replicated
Inputs may be any that keep to these rules, and one draw needn't show every extreme that they name: `parent`: each entry names a coarse token of the same frame; a token of level l is drawn with weight l + 1.
All inputs are finite; a program needn't handle non-finite values.
Results may differ from a plain program's by a relative error of at most 0.025.
Values may be sent and summed in bfloat16 or wider, within the bound.
A program may use at most 128 MiB of HBM per device.

v0:
```python
import functools
import math
import jax
import jax.numpy as jnp
from jax import lax
from jax.sharding import PartitionSpec as P

HEADS = 12
BLK = 4
LEVELS = 3


def as_sent(shard):
    return jax.tree.map(lambda a: a.astype(jnp.bfloat16) if a.dtype == jnp.float32 else a, shard)


def attend_forward(queries, key_rows, values, score_scale, query_form, key_form, score_form):
    scores = (
        jnp.einsum(
            query_form + "," + key_form + "->" + score_form,
            queries,
            key_rows,
            preferred_element_type=jnp.float32,
        )
        * score_scale
    )
    weights = jax.nn.softmax(scores, axis=-1)
    rounded = weights.astype(jnp.bfloat16)
    attended = jnp.einsum(
        score_form + "," + key_form + "->" + query_form,
        rounded,
        values,
        preferred_element_type=jnp.float32,
    )
    return attended.astype(jnp.bfloat16)


def attend_grads(
    weights,
    rounded,
    queries,
    key_rows,
    values,
    grad_out,
    score_scale,
    query_form,
    key_form,
    score_form,
):
    grad_values = jnp.einsum(
        score_form + "," + query_form + "->" + key_form,
        rounded,
        grad_out,
        preferred_element_type=jnp.float32,
    ).astype(jnp.bfloat16)
    grad_weights = jnp.einsum(
        query_form + "," + key_form + "->" + score_form,
        grad_out,
        values,
        preferred_element_type=jnp.float32,
    )
    inner = jnp.sum(weights * grad_weights, axis=-1, keepdims=True)
    grad_scores = (weights * (grad_weights - inner) * score_scale).astype(jnp.bfloat16)
    grad_queries = jnp.einsum(
        score_form + "," + key_form + "->" + query_form,
        grad_scores,
        key_rows,
        preferred_element_type=jnp.float32,
    ).astype(jnp.bfloat16)
    grad_keys = jnp.einsum(
        score_form + "," + query_form + "->" + key_form,
        grad_scores,
        queries,
        preferred_element_type=jnp.float32,
    ).astype(jnp.bfloat16)
    return (grad_queries, grad_keys, grad_values)


def attend_backward(
    queries, key_rows, values, grad_out, score_scale, query_form, key_form, score_form
):
    scores = (
        jnp.einsum(
            query_form + "," + key_form + "->" + score_form,
            queries,
            key_rows,
            preferred_element_type=jnp.float32,
        )
        * score_scale
    )
    weights = jax.nn.softmax(scores, axis=-1)
    rounded = weights.astype(jnp.bfloat16)
    return attend_grads(
        weights,
        rounded,
        queries,
        key_rows,
        values,
        grad_out,
        score_scale,
        query_form,
        key_form,
        score_form,
    )


def take_rows(table_rows, row_ids):
    return jnp.take(table_rows, row_ids, axis=0)


def rows_to_batch(tensor, head_dim):
    return tensor.reshape(tensor.shape[1], tensor.shape[2], -1, head_dim)


def batch_to_rows(tensor):
    return tensor.reshape(1, tensor.shape[0], tensor.shape[1], -1)


def columns_to_batch(tensor, head_dim):
    return tensor.reshape(tensor.shape[0], tensor.shape[1], tensor.shape[3], -1, head_dim)


def batch_to_columns(tensor):
    return tensor.reshape(tensor.shape[0], tensor.shape[1], 1, tensor.shape[2], -1)


def to_row_groups(tensor, groups):
    return tensor.reshape(groups, -1, tensor.shape[2], tensor.shape[3])


def to_column_groups(tensor, groups):
    return tensor.reshape(tensor.shape[0], tensor.shape[1], groups, -1, tensor.shape[3])


def local(
    fine_tokens,
    parent,
    coarse_tokens,
    tile_level,
    level_table,
    norm_gain,
    qkv_weight,
    out_weight,
    cotangent,
):
    frame_count, row_count, column_count, model_dim = fine_tokens.shape
    row_groups = lax.axis_size("fx")
    column_groups = lax.axis_size("fy")
    owners_dev = coarse_tokens.shape[1]
    half_width = model_dim // 2
    head_dim = model_dim // HEADS
    score_scale = head_dim ** (-0.5)
    block_count = column_count // BLK
    token_shape = (frame_count, row_count, column_count, half_width)
    level_onehot = (tile_level[:, :, None] == jnp.arange(LEVELS, dtype=jnp.int32)).astype(
        jnp.float32
    )
    level_add = jnp.sum(level_onehot[:, :, :, None] * level_table[None, None, :, :], axis=2)
    summary = (coarse_tokens.astype(jnp.float32) + level_add).astype(jnp.bfloat16)
    shard_piece = lax.all_gather(summary, "fx", axis=1, tiled=True)
    piece_rows = shard_piece.shape[1]
    inside = (parent >= 0) & (parent < piece_rows)
    local_index = jnp.clip(parent, 0, piece_rows - 1)
    picked = jax.vmap(take_rows)(shard_piece, local_index)
    read_rows = jnp.where(inside[..., None], picked.astype(jnp.float32), 0.0)
    spread = jnp.broadcast_to(
        read_rows[:, :, :, None, :], (frame_count, row_count, block_count, BLK, model_dim)
    )
    residual = fine_tokens.astype(jnp.float32) + spread.reshape(
        frame_count, row_count, column_count, model_dim
    )
    inv_rms = lax.rsqrt(jnp.mean(residual * residual, axis=-1, keepdims=True) + 1e-06)
    normed_pre = residual * inv_rms
    normed = (normed_pre * norm_gain).astype(jnp.bfloat16)
    flat_normed = normed.reshape(-1, model_dim)
    projected = jnp.dot(flat_normed, qkv_weight, preferred_element_type=jnp.float32).astype(
        jnp.bfloat16
    )
    projected = projected.reshape(frame_count, row_count, column_count, 3 * model_dim)
    row_query = projected[..., 0:half_width]
    column_query = projected[..., half_width:model_dim]
    row_key = projected[..., model_dim : model_dim + half_width]
    column_key = projected[..., model_dim + half_width : 2 * model_dim]
    row_value = projected[..., 2 * model_dim : 2 * model_dim + half_width]
    column_value = projected[..., 2 * model_dim + half_width : 3 * model_dim]
    flat_cot = cotangent.reshape(-1, model_dim)
    grad_att = jnp.dot(flat_cot, out_weight.T, preferred_element_type=jnp.float32).astype(
        jnp.bfloat16
    )
    grad_att = grad_att.reshape(frame_count, row_count, column_count, model_dim)
    row_grad_out = grad_att[..., 0:half_width]
    column_grad_out = grad_att[..., half_width:model_dim]
    queries = lax.all_to_all(
        to_row_groups(row_query, row_groups), "fx", split_axis=0, concat_axis=2, tiled=True
    )
    key_rows = lax.all_to_all(
        to_row_groups(row_key, row_groups), "fx", split_axis=0, concat_axis=2, tiled=True
    )
    values = lax.all_to_all(
        to_row_groups(row_value, row_groups), "fx", split_axis=0, concat_axis=2, tiled=True
    )
    attended_rows = attend_forward(
        rows_to_batch(queries, head_dim),
        rows_to_batch(key_rows, head_dim),
        rows_to_batch(values, head_dim),
        score_scale,
        "bqhd",
        "bkhd",
        "bhqk",
    )
    row_out = lax.all_to_all(
        batch_to_rows(attended_rows), "fx", split_axis=2, concat_axis=0, tiled=True
    )
    row_out = row_out.reshape(token_shape)
    queries = lax.all_to_all(
        to_column_groups(column_query, column_groups), "fy", split_axis=2, concat_axis=1, tiled=True
    )
    key_rows = lax.all_to_all(
        to_column_groups(column_key, column_groups), "fy", split_axis=2, concat_axis=1, tiled=True
    )
    values = lax.all_to_all(
        to_column_groups(column_value, column_groups), "fy", split_axis=2, concat_axis=1, tiled=True
    )
    attended_columns = attend_forward(
        columns_to_batch(queries, head_dim),
        columns_to_batch(key_rows, head_dim),
        columns_to_batch(values, head_dim),
        score_scale,
        "fqchd",
        "fkchd",
        "fchqk",
    )
    column_out = lax.all_to_all(
        batch_to_columns(attended_columns), "fy", split_axis=1, concat_axis=2, tiled=True
    )
    column_out = column_out.reshape(token_shape)
    queries = lax.all_to_all(
        to_row_groups(row_query, row_groups), "fx", split_axis=0, concat_axis=2, tiled=True
    )
    key_rows = lax.all_to_all(
        to_row_groups(row_key, row_groups), "fx", split_axis=0, concat_axis=2, tiled=True
    )
    values = lax.all_to_all(
        to_row_groups(row_value, row_groups), "fx", split_axis=0, concat_axis=2, tiled=True
    )
    grad_rows = lax.all_to_all(
        to_row_groups(row_grad_out, row_groups), "fx", split_axis=0, concat_axis=2, tiled=True
    )
    grads = attend_backward(
        rows_to_batch(queries, head_dim),
        rows_to_batch(key_rows, head_dim),
        rows_to_batch(values, head_dim),
        rows_to_batch(grad_rows, head_dim),
        score_scale,
        "bqhd",
        "bkhd",
        "bhqk",
    )
    row_back = (
        lax.all_to_all(batch_to_rows(grads[0]), "fx", split_axis=2, concat_axis=0, tiled=True),
        lax.all_to_all(batch_to_rows(grads[1]), "fx", split_axis=2, concat_axis=0, tiled=True),
        lax.all_to_all(batch_to_rows(grads[2]), "fx", split_axis=2, concat_axis=0, tiled=True),
    )
    queries = lax.all_to_all(
        to_column_groups(column_query, column_groups), "fy", split_axis=2, concat_axis=1, tiled=True
    )
    key_rows = lax.all_to_all(
        to_column_groups(column_key, column_groups), "fy", split_axis=2, concat_axis=1, tiled=True
    )
    values = lax.all_to_all(
        to_column_groups(column_value, column_groups), "fy", split_axis=2, concat_axis=1, tiled=True
    )
    grad_columns = lax.all_to_all(
        to_column_groups(column_grad_out, column_groups),
        "fy",
        split_axis=2,
        concat_axis=1,
        tiled=True,
    )
    grads = attend_backward(
        columns_to_batch(queries, head_dim),
        columns_to_batch(key_rows, head_dim),
        columns_to_batch(values, head_dim),
        columns_to_batch(grad_columns, head_dim),
        score_scale,
        "fqchd",
        "fkchd",
        "fchqk",
    )
    column_back = (
        lax.all_to_all(batch_to_columns(grads[0]), "fy", split_axis=1, concat_axis=2, tiled=True),
        lax.all_to_all(batch_to_columns(grads[1]), "fy", split_axis=1, concat_axis=2, tiled=True),
        lax.all_to_all(batch_to_columns(grads[2]), "fy", split_axis=1, concat_axis=2, tiled=True),
    )
    attended = jnp.concatenate([row_out, column_out], axis=-1)
    flat_att = attended.reshape(-1, model_dim)
    out_proj = jnp.dot(flat_att, out_weight, preferred_element_type=jnp.float32)
    mixed = (residual + out_proj.reshape(frame_count, row_count, column_count, model_dim)).astype(
        jnp.bfloat16
    )
    grad_out_local = jnp.dot(flat_att.T, flat_cot, preferred_element_type=jnp.float32)
    pieces = []
    for which in range(3):
        pieces.append(row_back[which].reshape(token_shape))
        pieces.append(column_back[which].reshape(token_shape))
    grad_projected = jnp.concatenate(pieces, axis=-1).reshape(-1, 3 * model_dim)
    grad_normed = jnp.dot(grad_projected, qkv_weight.T, preferred_element_type=jnp.float32)
    grad_qkv_local = jnp.dot(flat_normed.T, grad_projected, preferred_element_type=jnp.float32)
    flat_pre = normed_pre.reshape(-1, model_dim)
    grad_gain_local = jnp.sum(grad_normed * flat_pre, axis=0)
    grad_pre = grad_normed * norm_gain
    flat_inv = inv_rms.reshape(-1, 1)
    grad_residual = flat_inv * (
        grad_pre - flat_pre * jnp.mean(grad_pre * flat_pre, axis=-1, keepdims=True)
    ) + flat_cot.astype(jnp.float32)
    grad_fine = grad_residual.astype(jnp.bfloat16).reshape(
        frame_count, row_count, column_count, model_dim
    )
    block_grad = (
        grad_residual.reshape(frame_count, row_count, block_count, BLK, model_dim)
        .sum(axis=3)
        .reshape(frame_count, -1, model_dim)
    )
    parent_flat = parent.reshape(frame_count, -1)
    coarse_total = owners_dev * row_groups
    segment_rows = functools.partial(jax.ops.segment_sum, num_segments=coarse_total)
    dense_sum = jax.vmap(segment_rows)(block_grad, parent_flat)
    owned_rows = jax.tree.map(
        lambda part: part.astype(jnp.float32),
        lax.psum_scatter(as_sent(dense_sum), "fx", scatter_dimension=1, tiled=True),
    )
    grad_coarse = jax.tree.map(
        lambda part: part.astype(jnp.float32), lax.psum(as_sent(owned_rows), "fy")
    )
    level_part = jnp.sum(level_onehot[:, :, :, None] * grad_coarse[:, :, None, :], axis=(0, 1))
    grad_level = lax.psum(level_part, ("dp", "fx"))
    summed = (
        lax.psum(grad_qkv_local.astype(jnp.bfloat16), ("fy", "fx")).astype(jnp.float32),
        lax.psum(grad_out_local.astype(jnp.bfloat16), ("fy", "fx")).astype(jnp.float32),
        lax.psum(grad_gain_local.astype(jnp.bfloat16), ("fy", "fx")).astype(jnp.float32),
    )
    shares = (
        lax.psum_scatter(
            summed[0].astype(jnp.bfloat16), "dp", scatter_dimension=0, tiled=True
        ).astype(jnp.float32),
        lax.psum_scatter(
            summed[1].astype(jnp.bfloat16), "dp", scatter_dimension=0, tiled=True
        ).astype(jnp.float32),
        lax.psum_scatter(
            summed[2].astype(jnp.bfloat16), "dp", scatter_dimension=0, tiled=True
        ).astype(jnp.float32),
    )
    total_tokens = (
        frame_count * row_count * column_count * lax.axis_size("dp") * column_groups * row_groups
    )
    grad_scale = 1.0 / math.sqrt(total_tokens)
    return (
        mixed,
        grad_fine,
        grad_coarse,
        shares[0] * grad_scale,
        shares[1] * grad_scale,
        shares[2] * grad_scale,
        grad_level * grad_scale,
    )


def solution(mesh):
    return jax.shard_map(
        local,
        mesh=mesh,
        in_specs=(
            P("dp", "fy", "fx", None),
            P("dp", "fy", "fx"),
            P("dp", "fx", None),
            P("dp", "fx"),
            P(),
            P(),
            P(),
            P(),
            P("dp", "fy", "fx", None),
        ),
        out_specs=(
            P("dp", "fy", "fx", None),
            P("dp", "fy", "fx", None),
            P("dp", "fx", None),
            P("dp", None),
            P("dp", None),
            P("dp"),
            P(),
        ),
        check_vma=False,
    )
```

profile of v0, /device:TPU:0, one launch (start us, length us, event | category | flops | bytes accessed | tf_op | source)
XLA Modules:
  0.0 606.6 jit_solution(17159746881032802387)
XLA Ops:
  12.2 5.3 all-to-all-start.10
  23.4 31.8 %all_gather.3 = bf16[1,512,768]{2,1,0:T(8,128)(2,1)} all-gather(bf16[1,64,768]{2,1,0:T(8,128)(2,1)S(1)} %fusion.66), channel_id=1, replica_groups=mesh['dp'=4,'fy'=4,'fx'=8] {'fx'}, dimensions={1}, use_global_device_ids=true | all-gather | bytes 884736 | tf_op jit(solution)/shard_map/all_gather | solution.py:160
  71.1 5.4 all-to-all-start.6
  78.3 7.2 %all-to-all-done.6 = bf16[1,16,4,8,384]{4,3,1,0,2:T(8,128)(2,1)} async-done(((bf16[1,16,4,8,384]{4,3,1,0,2:T(8,128)(2,1)}), bf16[1,16,4,8,384]{4,3,1,0,2:T(8,128)(2,1)}, u32[]{:S(2)}, u32[]{:S(2)}) %all-to-all-start.6) | async-done | bytes 393248 | tf_op jit(solution)/shard_map/all_to_all | solution.py:218
  91.4 7.2 %all-to-all-done.5 = bf16[1,16,4,8,384]{4,3,1,0,2:T(8,128)(2,1)} async-done(((bf16[1,16,4,8,384]{4,3,1,0,2:T(8,128)(2,1)}), bf16[1,16,4,8,384]{4,3,1,0,2:T(8,128)(2,1)}, u32[]{:S(2)}, u32[]{:S(2)}) %all-to-all-start.5) | async-done | bytes 393248 | tf_op jit(solution)/shard_map/all_to_all | solution.py:215
  98.6 13.2 %all_to_all.270 = bf16[1,16,4,8,384]{4,3,1,0,2:T(8,128)(2,1)} all-to-all(bf16[1,16,4,8,384]{4,3,1,0,2:T(8,128)(2,1)} %copy.222), channel_id=1, replica_groups=mesh['dp'=4,'fy'=4,'fx'=8] {'fy'}, dimensions={2} | all-to-all | bytes 786432 | tf_op jit(solution)/shard_map/all_to_all | solution.py:221
  111.8 12.7 %all_to_all.271 = bf16[8,2,32,384]{3,2,1,0:T(8,128)(2,1)} all-to-all(bf16[8,2,32,384]{3,2,1,0:T(8,128)(2,1)} %bitcast.260), channel_id=1, replica_groups=mesh['dp'=4,'fy'=4,'fx'=8] {'fx'}, dimensions={0} | all-to-all | bytes 786432 | tf_op jit(solution)/shard_map/all_to_all | solution.py:246
  124.5 11.1 %all_to_all.272 = bf16[8,2,32,384]{3,2,1,0:T(8,128)(2,1)} all-to-all(bf16[8,2,32,384]{3,2,1,0:T(8,128)(2,1)S(1)} %bitcast.251), channel_id=1, replica_groups=mesh['dp'=4,'fy'=4,'fx'=8] {'fx'}, dimensions={0} | all-to-all | bytes 786432 | tf_op jit(solution)/shard_map/all_to_all | solution.py:196
  160.7 6.1 %all-to-all-start = ((bf16[8,2,32,384]{3,2,1,0:T(8,128)(2,1)}), bf16[8,2,32,384]{3,2,1,0:T(8,128)(2,1)}, u32[]{:S(2)}, u32[]{:S(2)}) async-start(bf16[8,2,32,384]{3,2,1,0:T(8,128)(2,1)} %bitcast.249), calls=%async_computation | async-start | bytes 786432 | tf_op jit(solution)/shard_map/all_to_all | solution.py:199
  187.0 4.6 fusion.40
  216.9 4.8 all-to-all-start.13
  243.8 5.9 all-to-all-start.14
  253.1 6.6 %fusion.43 = bf16[2,6,64,256]{3,2,1,0:T(8,128)(2,1)} fusion(bf16[2,256,6,64]{1,3,2,0:T(8,128)(2,1)} %reshape.445, f32[2,6,256,256]{2,3,1,0:T(8,128)} %fusion.91, f32[2,6,256,256]{2,3,1,0:T(8,128)} %get-tuple-element.28, f32[2,6,256]{2,1,0:T(8,128)} %get-tuple-element.27), kind=kOutput, calls=%fused_computation.49 | convolution fusion | flops 106368256 | bytes 7090176 | tf_op jit(solution)/shard_map/bhqk,bkhd->bqhd/dot_general | solution.py:64
  261.6 5.7 all-to-all-start.9
  267.3 6.6 %fusion.46 = bf16[2,6,64,256]{3,2,1,0:T(8,128)(2,1)} fusion(bf16[2,256,6,64]{1,3,2,0:T(8,128)(2,1)} %reshape.444, f32[2,6,256,256]{2,3,1,0:T(8,128)} %fusion.91, f32[2,6,256,256]{2,3,1,0:T(8,128)} %get-tuple-element.28, f32[2,6,256]{2,1,0:T(8,128)} %get-tuple-element.27), kind=kOutput, calls=%fused_computation.50 | convolution fusion | flops 106368256 | bytes 7090176 | tf_op jit(solution)/shard_map/bhqk,bqhd->bkhd/dot_general | solution.py:70
  275.8 5.7 all-to-all-start.12
  314.2 6.9 %all-to-all-done.7 = bf16[1,64,1,8,384]{4,3,2,0,1:T(8,128)(2,1)S(1)} async-done(((bf16[1,64,1,8,384]{4,3,2,0,1:T(8,128)(2,1)}), bf16[1,64,1,8,384]{4,3,2,0,1:T(8,128)(2,1)S(1)}, u32[]{:S(2)}, u32[]{:S(2)}) %all-to-all-start.7) | async-done | bytes 393248 | tf_op jit(solution)/shard_map/all_to_all | solution.py:233
  321.1 5.1 all-to-all-start.3
  326.3 9.3 %all-to-all-done.3 = bf16[1,2,256,384]{3,1,0,2:T(2,128)(2,1)S(1)} async-done(((bf16[1,2,256,384]{3,1,0,2:T(2,128)(2,1)}), bf16[1,2,256,384]{3,1,0,2:T(2,128)(2,1)S(1)}, u32[]{:S(2)}, u32[]{:S(2)}) %all-to-all-start.3) | async-done | bytes 393248 | tf_op jit(solution)/shard_map/all_to_all | solution.py:211
  337.6 6.4 %reduce-scatter.4.cloned.1.call-done = bf16[1,64,768]{2,1,0:T(8,128)(2,1)} async-done(((bf16[1,512,768]{2,1,0:T(8,128)(2,1)}), bf16[1,64,768]{2,1,0:T(8,128)(2,1)}) %reduce-scatter.4.cloned.1.call-update) | async-done | bytes 98320 | tf_op jit(solution)/shard_map/reduce_scatter | solution.py:330
  352.4 5.5 bitcast_convert_fusion
  359.8 10.5 %all-reduce = bf16[768]{0:T(1024)(128)(2,1)S(1)} all-reduce(bf16[768]{0:T(1024)(128)(2,1)S(1)} %get-tuple-element.7), channel_id=5, replica_groups=mesh['dp'=4,'fy'=4,'fx'=8] {'dp'}, use_global_device_ids=true, to_apply=%region_19.20.clone | all-reduce | flops 768 | bytes 3072
  370.4 62.7 %psum.42 = bf16[192]{0:T(256)(128)(2,1)S(1)} all-reduce(bf16[192]{0:T(256)(128)(2,1)S(1)} %dynamic-slice.1), channel_id=1, replica_groups=mesh['dp'=4,'fy'=4,'fx'=8] {'fy','fx'}, use_global_device_ids=true, to_apply=%region_18.19 | all-reduce | flops 192 | bytes 768 | tf_op jit(solution)/shard_map/psum | solution.py:340
  439.3 154.4 %psum.39 = f32[3,768]{1,0:T(4,128)S(1)} all-reduce(f32[3,768]{1,0:T(4,128)S(1)} %multiply_reduce_fusion.4), channel_id=1, replica_groups=mesh['dp'=4,'fy'=4,'fx'=8] {'dp','fx'}, use_global_device_ids=true, to_apply=%region_21.22 | all-reduce | flops 2304 | bytes 18432 | tf_op jit(solution)/shard_map/psum | solution.py:336
  (193 shorter events, 189.0 us)
Async XLA Ops:
  8.0 59.0 %copy-start = (bf16[768,2304]{1,0:T(8,128)(2,1)S(1)}, bf16[768,2304]{1,0:T(8,128)(2,1)}, u32[]{:S(2)}) copy-start(bf16[768,2304]{1,0:T(8,128)(2,1)} %param.15) | copy-start | bytes 10616836
  12.2 58.9 %all-to-all-start.10 = ((bf16[1,16,4,8,384]{4,3,1,0,2:T(8,128)(2,1)}), bf16[1,16,4,8,384]{4,3,1,0,2:T(8,128)(2,1)}, u32[]{:S(2)}, u32[]{:S(2)}) async-start(bf16[1,16,4,8,384]{4,3,1,0,2:T(8,128)(2,1)} %copy.239), calls=%async_computation.10 | async-start | bytes 786432 | tf_op jit(solution)/shard_map/all_to_all | solution.py:273
  71.1 14.4 %all-to-all-start.6 = ((bf16[1,16,4,8,384]{4,3,1,0,2:T(8,128)(2,1)}), bf16[1,16,4,8,384]{4,3,1,0,2:T(8,128)(2,1)}, u32[]{:S(2)}, u32[]{:S(2)}) async-start(bf16[1,16,4,8,384]{4,3,1,0,2:T(8,128)(2,1)} %copy.224), calls=%async_computation.6 | async-start | bytes 786432 | tf_op jit(solution)/shard_map/all_to_all | solution.py:218
  85.5 13.1 %all-to-all-start.5 = ((bf16[1,16,4,8,384]{4,3,1,0,2:T(8,128)(2,1)}), bf16[1,16,4,8,384]{4,3,1,0,2:T(8,128)(2,1)}, u32[]{:S(2)}, u32[]{:S(2)}) async-start(bf16[1,16,4,8,384]{4,3,1,0,2:T(8,128)(2,1)} %copy.223), calls=%async_computation.5 | async-start | bytes 786432 | tf_op jit(solution)/shard_map/all_to_all | solution.py:215
  98.6 25.9 %copy-start.14 = (bf16[1,16,32,384]{3,2,1,0:T(8,128)(2,1)S(1)}, bf16[1,16,32,384]{3,2,1,0:T(8,128)(2,1)}, u32[]{:S(2)}) copy-start(bf16[1,16,32,384]{3,2,1,0:T(8,128)(2,1)} %get-tuple-element.15) | copy-start | bytes 1179652
  135.6 25.2 %all-to-all-start.1 = ((bf16[8,2,32,384]{3,2,1,0:T(8,128)(2,1)}), bf16[8,2,32,384]{3,2,1,0:T(8,128)(2,1)}, u32[]{:S(2)}, u32[]{:S(2)}) async-start(bf16[8,2,32,384]{3,2,1,0:T(8,128)(2,1)} %bitcast.250), calls=%async_computation.1 | async-start | bytes 786432 | tf_op jit(solution)/shard_map/all_to_all | solution.py:193
  160.7 16.9 %all-to-all-start = ((bf16[8,2,32,384]{3,2,1,0:T(8,128)(2,1)}), bf16[8,2,32,384]{3,2,1,0:T(8,128)(2,1)}, u32[]{:S(2)}, u32[]{:S(2)}) async-start(bf16[8,2,32,384]{3,2,1,0:T(8,128)(2,1)} %bitcast.249), calls=%async_computation | async-start | bytes 786432 | tf_op jit(solution)/shard_map/all_to_all | solution.py:199
  177.6 39.3 %all-to-all-start.11 = ((bf16[1,64,1,8,384]{4,3,2,0,1:T(8,128)(2,1)}), bf16[1,64,1,8,384]{4,3,2,0,1:T(8,128)(2,1)}, u32[]{:S(2)}, u32[]{:S(2)}) async-start(bf16[1,64,1,8,384]{4,3,2,0,1:T(8,128)(2,1)} %copy.244), calls=%async_computation.11 | async-start | bytes 786432 | tf_op jit(solution)/shard_map/all_to_all | solution.py:291
  216.9 13.8 %all-to-all-start.13 = ((bf16[1,64,1,8,384]{4,3,2,0,1:T(8,128)(2,1)}), bf16[1,64,1,8,384]{4,3,2,0,1:T(8,128)(2,1)}, u32[]{:S(2)}, u32[]{:S(2)}) async-start(bf16[1,64,1,8,384]{4,3,2,0,1:T(8,128)(2,1)} %copy.253), calls=%async_computation.13 | async-start | bytes 786432 | tf_op jit(solution)/shard_map/all_to_all | solution.py:292
  230.7 13.1 %all-to-all-start.15 = ((bf16[1,64,1,8,384]{4,3,2,0,1:T(8,128)(2,1)}), bf16[1,64,1,8,384]{4,3,2,0,1:T(8,128)(2,1)}, u32[]{:S(2)}, u32[]{:S(2)}) async-start(bf16[1,64,1,8,384]{4,3,2,0,1:T(8,128)(2,1)} %copy.262), calls=%async_computation.15 | async-start | bytes 786432 | tf_op jit(solution)/shard_map/all_to_all | solution.py:293
  243.8 17.8 %all-to-all-start.14 = ((bf16[1,2,256,384]{3,1,0,2:T(2,128)(2,1)}), bf16[1,2,256,384]{3,1,0,2:T(2,128)(2,1)}, u32[]{:S(2)}, u32[]{:S(2)}) async-start(bf16[1,2,256,384]{3,1,0,2:T(2,128)(2,1)} %copy.257), calls=%async_computation.14 | async-start | bytes 786432 | tf_op jit(solution)/shard_map/all_to_all | solution.py:262
  261.6 14.2 %all-to-all-start.9 = ((bf16[1,2,256,384]{3,1,0,2:T(2,128)(2,1)}), bf16[1,2,256,384]{3,1,0,2:T(2,128)(2,1)}, u32[]{:S(2)}, u32[]{:S(2)}) async-start(bf16[1,2,256,384]{3,1,0,2:T(2,128)(2,1)} %copy.236), calls=%async_computation.9 | async-start | bytes 786432 | tf_op jit(solution)/shard_map/all_to_all | solution.py:260
  275.8 16.9 %all-to-all-start.12 = ((bf16[1,2,256,384]{3,1,0,2:T(2,128)(2,1)}), bf16[1,2,256,384]{3,1,0,2:T(2,128)(2,1)}, u32[]{:S(2)}, u32[]{:S(2)}) async-start(bf16[1,2,256,384]{3,1,0,2:T(2,128)(2,1)} %copy.248), calls=%async_computation.12 | async-start | bytes 786432 | tf_op jit(solution)/shard_map/all_to_all | solution.py:261
  281.6 62.5 %reduce-scatter.4.cloned.1.call-start = ((), (), s32[]{:S(2)}) async-start(), calls=%async_computation.19 | async-start | bytes 884736 | tf_op jit(solution)/shard_map/reduce_scatter | solution.py:330
  307.3 13.8 %all-to-all-start.7 = ((bf16[1,64,1,8,384]{4,3,2,0,1:T(8,128)(2,1)}), bf16[1,64,1,8,384]{4,3,2,0,1:T(8,128)(2,1)S(1)}, u32[]{:S(2)}, u32[]{:S(2)}) async-start(bf16[1,64,1,8,384]{4,3,2,0,1:T(8,128)(2,1)} %copy.229), calls=%async_computation.7 | async-start | bytes 786432 | tf_op jit(solution)/shard_map/all_to_all | solution.py:233
  314.2 21.5 %copy-start.20 = (bf16[1,16,32,768]{3,2,1,0:T(8,128)(2,1)S(1)}, bf16[1,16,32,768]{3,2,1,0:T(8,128)(2,1)}, u32[]{:S(2)}) copy-start(bf16[1,16,32,768]{3,2,1,0:T(8,128)(2,1)} %param.17) | copy-start | bytes 2359300
  321.1 14.5 %all-to-all-start.3 = ((bf16[1,2,256,384]{3,1,0,2:T(2,128)(2,1)}), bf16[1,2,256,384]{3,1,0,2:T(2,128)(2,1)S(1)}, u32[]{:S(2)}, u32[]{:S(2)}) async-start(bf16[1,2,256,384]{3,1,0,2:T(2,128)(2,1)} %copy.219), calls=%async_computation.3 | async-start | bytes 786432 | tf_op jit(solution)/shard_map/all_to_all | solution.py:211
  326.2 110.4 %all-reduce.5.cloned.1.call-start = ((), (), s32[]{:S(2)}) async-start(), calls=%async_computation.20 | async-start | bytes 196608 | tf_op jit(solution)/shard_map/psum | solution.py:333
  337.6 9.5 %copy-start.8 = (bf16[8,1,2,32,384]{4,3,2,0,1:T(8,128)(2,1)S(1)}, bf16[8,1,2,32,384]{4,3,2,0,1:T(8,128)(2,1)}, u32[]{:S(2)}) copy-start(bf16[8,1,2,32,384]{4,3,2,0,1:T(8,128)(2,1)} %copy-done.7) | copy-start | bytes 1179652
  344.0 94.2 %reduce-scatter.8.cloned.1.call-start = ((), (), s32[]{:S(2)}) async-start(), calls=%async_computation.22 | async-start | bytes 1474560 | tf_op jit(solution)/shard_map/reduce_scatter | solution.py:346
  345.0 93.2 %reduce-scatter.6.cloned.1.call-start = ((), (), s32[]{:S(2)}) async-start(), calls=%async_computation.21 | async-start | bytes 4423680 | tf_op jit(solution)/shard_map/reduce_scatter | solution.py:343
  357.9 75.8 %copy-start.3 = (f32[1,16,32,768]{3,2,1,0:T(8,128)S(1)}, f32[1,16,32,768]{3,2,1,0:T(8,128)}, u32[]{:S(2)}) copy-start(f32[1,16,32,768]{3,2,1,0:T(8,128)} %broadcast_in_dim.39) | copy-start | bytes 4718596
  357.9 75.8 %copy-start.13 = (bf16[1,16,32,768]{3,2,1,0:T(8,128)(2,1)S(1)}, bf16[1,16,32,768]{3,2,1,0:T(8,128)(2,1)}, u32[]{:S(2)}) copy-start(bf16[1,16,32,768]{3,2,1,0:T(8,128)(2,1)} %param.9) | copy-start | bytes 2359300
  357.9 236.4 %all-reduce.7.cloned.1.call-start = ((), (), s32[]{:S(2)}) async-start(), calls=%async_computation.23 | async-start | bytes 2359296 | tf_op jit(solution)/shard_map/psum | solution.py:338
  (24 other events, 71.7 us)
Sparse Core Ops, SparseCore 0:
  303.7 40.2 reduce-scatter.3
  346.5 38.8 all-reduce.4
Sparse Core Ops, SparseCore 1:
  347.5 23.0 reduce-scatter.7
  372.9 41.1 reduce-scatter.5
  438.3 101.2 all-reduce.6
where the time goes:
time: 618 us; the launch traced here: 607 us
  blocking collectives  296 us (48%)
  local copies, waits for them, and re-layouts  97.6 us (16%)
  matrix products  65.2 us (11%)
  starting transfers between devices  64.2 us (10%)
  waiting for transfers between devices  45.4 us (7%)
  other arithmetic  20.7 us (3%)
  between operations  17 us (3%)
    psum x1, blocking collectives, local(): grad_level = lax.psum(level_part, ('dp', 'fx'))  154 us
    psum x1, blocking collectives, local(): lax.psum(grad_gain_local.astype(jnp.bfloat16), ('fy', 'fx'))  62.7 us
    all_gather x1, blocking collectives, local(): shard_piece = lax.all_gather(summary, 'fx', axis=1, tiled=True)  31.8 us
    reshape x8, local copies, waits for them, and re-layouts, rows_to_batch(): return tensor.reshape(tensor.shape[1], tensor.shape[2], -1, head_dim)  23 us
    another operation x7, local copies, waits for them, and re-layouts  17.7 us
    all_to_all x1, blocking collectives, local(): lax.all_to_all(to_column_groups(column_value, column_groups), 'fy', split...  13.2 us
    all_to_all x1, blocking collectives, local(): lax.all_to_all(to_row_groups(row_grad_out, row_groups), 'fx', split_axis=...  12.7 us
  transfers between devices with their start and end apart: 18, of which 7 were waited for; matrix products, arithmetic and copies ran while one was open for 27% of the time, Pallas kernels for 0%

commit v1 on v0

--- a/solution.py
+++ b/solution.py
@@ -333,7 +333,8 @@
         lambda part: part.astype(jnp.float32), lax.psum(as_sent(owned_rows), "fy")
     )
     level_part = jnp.sum(level_onehot[:, :, :, None] * grad_coarse[:, :, None, :], axis=(0, 1))
-    grad_level = lax.psum(level_part, ("dp", "fx"))
+    half = lax.psum(level_part, "dp")
+    grad_level = lax.psum(half, "fx")
     summed = (
         lax.psum(grad_qkv_local.astype(jnp.bfloat16), ("fy", "fx")).astype(jnp.float32),
         lax.psum(grad_out_local.astype(jnp.bfloat16), ("fy", "fx")).astype(jnp.float32),

time: 618 us -> 563 us (0.911)
  the two profiles are of different devices: /device:TPU:0 before, /device:TPU:1 now
where the time goes in v1:
time: 563 us; the launch traced here: 552 us
  blocking collectives  170 us (30%)
  waiting for transfers between devices  105 us (19%)
  local copies, waits for them, and re-layouts  97.7 us (17%)
  starting transfers between devices  76.6 us (14%)
  matrix products  65.2 us (12%)
  other arithmetic  20.7 us (4%)
  between operations  17 us (3%)
    psum x1, waiting for transfers between devices, local(): lax.psum(grad_qkv_local.astype(jnp.bfloat16), ('fy', 'fx'))  70 us
    psum x1, blocking collectives, local(): lax.psum(grad_gain_local.astype(jnp.bfloat16), ('fy', 'fx'))  64.7 us
    all_gather x1, blocking collectives, local(): shard_piece = lax.all_gather(summary, 'fx', axis=1, tiled=True)  26.4 us
    psum x1, blocking collectives, local(): grad_level = lax.psum(half, 'fx')  23.7 us
    reshape x8, local copies, waits for them, and re-layouts, rows_to_batch(): return tensor.reshape(tensor.shape[1], tensor.shape[2], -1, head_dim)  23.1 us
    another operation x7, local copies, waits for them, and re-layouts  17.8 us
    all_to_all x1, blocking collectives, local(): lax.all_to_all(to_column_groups(column_value, column_groups), 'fy', split...  13.1 us
    all_to_all x1, blocking collectives, local(): lax.all_to_all(to_row_groups(row_grad_out, row_groups), 'fx', split_axis=...  11.8 us
  transfers between devices with their start and end apart: 18, of which 8 were waited for; matrix products, arithmetic and copies ran while one was open for 29% of the time, Pallas kernels for 0%

profile of v1, /device:TPU:1, one launch (start us, length us, event | category | flops | bytes accessed | tf_op | source)
XLA Modules:
  0.0 552.4 jit_solution(13026054582719284484)
XLA Ops:
  12.2 6.6 %all-to-all-start.10 = ((bf16[1,16,4,8,384]{4,3,1,0,2:T(8,128)(2,1)}), bf16[1,16,4,8,384]{4,3,1,0,2:T(8,128)(2,1)}, u32[]{:S(2)}, u32[]{:S(2)}) async-start(bf16[1,16,4,8,384]{4,3,1,0,2:T(8,128)(2,1)} %copy.239), calls=%async_computation.10 | async-start | bytes 786432 | tf_op jit(solution)/shard_map/all_to_all | solution.py:273
  24.7 26.4 %all_gather.3 = bf16[1,512,768]{2,1,0:T(8,128)(2,1)} all-gather(bf16[1,64,768]{2,1,0:T(8,128)(2,1)S(1)} %fusion.66), channel_id=1, replica_groups=mesh['dp'=4,'fy'=4,'fx'=8] {'fx'}, dimensions={1}, use_global_device_ids=true | all-gather | bytes 884736 | tf_op jit(solution)/shard_map/all_gather | solution.py:160
  67.1 10.8 %all-to-all-start.6 = ((bf16[1,16,4,8,384]{4,3,1,0,2:T(8,128)(2,1)}), bf16[1,16,4,8,384]{4,3,1,0,2:T(8,128)(2,1)}, u32[]{:S(2)}, u32[]{:S(2)}) async-start(bf16[1,16,4,8,384]{4,3,1,0,2:T(8,128)(2,1)} %copy.224), calls=%async_computation.6 | async-start | bytes 786432 | tf_op jit(solution)/shard_map/all_to_all | solution.py:218
  79.7 6.3 %all-to-all-done.6 = bf16[1,16,4,8,384]{4,3,1,0,2:T(8,128)(2,1)} async-done(((bf16[1,16,4,8,384]{4,3,1,0,2:T(8,128)(2,1)}), bf16[1,16,4,8,384]{4,3,1,0,2:T(8,128)(2,1)}, u32[]{:S(2)}, u32[]{:S(2)}) %all-to-all-start.6) | async-done | bytes 393248 | tf_op jit(solution)/shard_map/all_to_all | solution.py:218
  92.8 6.3 %all-to-all-done.5 = bf16[1,16,4,8,384]{4,3,1,0,2:T(8,128)(2,1)} async-done(((bf16[1,16,4,8,384]{4,3,1,0,2:T(8,128)(2,1)}), bf16[1,16,4,8,384]{4,3,1,0,2:T(8,128)(2,1)}, u32[]{:S(2)}, u32[]{:S(2)}) %all-to-all-start.5) | async-done | bytes 393248 | tf_op jit(solution)/shard_map/all_to_all | solution.py:215
  99.0 13.1 %all_to_all.270 = bf16[1,16,4,8,384]{4,3,1,0,2:T(8,128)(2,1)} all-to-all(bf16[1,16,4,8,384]{4,3,1,0,2:T(8,128)(2,1)} %copy.222), channel_id=1, replica_groups=mesh['dp'=4,'fy'=4,'fx'=8] {'fy'}, dimensions={2} | all-to-all | bytes 786432 | tf_op jit(solution)/shard_map/all_to_all | solution.py:221
  112.2 11.8 %all_to_all.271 = bf16[8,2,32,384]{3,2,1,0:T(8,128)(2,1)} all-to-all(bf16[8,2,32,384]{3,2,1,0:T(8,128)(2,1)} %bitcast.260), channel_id=1, replica_groups=mesh['dp'=4,'fy'=4,'fx'=8] {'fx'}, dimensions={0} | all-to-all | bytes 786432 | tf_op jit(solution)/shard_map/all_to_all | solution.py:246
  124.0 10.2 %all_to_all.272 = bf16[8,2,32,384]{3,2,1,0:T(8,128)(2,1)} all-to-all(bf16[8,2,32,384]{3,2,1,0:T(8,128)(2,1)S(1)} %bitcast.251), channel_id=1, replica_groups=mesh['dp'=4,'fy'=4,'fx'=8] {'fx'}, dimensions={0} | all-to-all | bytes 786432 | tf_op jit(solution)/shard_map/all_to_all | solution.py:196
  159.4 5.6 %all-to-all-start = ((bf16[8,2,32,384]{3,2,1,0:T(8,128)(2,1)}), bf16[8,2,32,384]{3,2,1,0:T(8,128)(2,1)}, u32[]{:S(2)}, u32[]{:S(2)}) async-start(bf16[8,2,32,384]{3,2,1,0:T(8,128)(2,1)} %bitcast.249), calls=%async_computation | async-start | bytes 786432 | tf_op jit(solution)/shard_map/all_to_all | solution.py:199
  175.7 7.4 %all-to-all-start.11 = ((bf16[1,64,1,8,384]{4,3,2,0,1:T(8,128)(2,1)}), bf16[1,64,1,8,384]{4,3,2,0,1:T(8,128)(2,1)}, u32[]{:S(2)}, u32[]{:S(2)}) async-start(bf16[1,64,1,8,384]{4,3,2,0,1:T(8,128)(2,1)} %copy.244), calls=%async_computation.11 | async-start | bytes 786432 | tf_op jit(solution)/shard_map/all_to_all | solution.py:291
  244.3 5.7 %all-to-all-start.14 = ((bf16[1,2,256,384]{3,1,0,2:T(2,128)(2,1)}), bf16[1,2,256,384]{3,1,0,2:T(2,128)(2,1)}, u32[]{:S(2)}, u32[]{:S(2)}) async-start(bf16[1,2,256,384]{3,1,0,2:T(2,128)(2,1)} %copy.257), calls=%async_computation.14 | async-start | bytes 786432 | tf_op jit(solution)/shard_map/all_to_all | solution.py:262
  253.3 6.6 %fusion.43 = bf16[2,6,64,256]{3,2,1,0:T(8,128)(2,1)} fusion(bf16[2,256,6,64]{1,3,2,0:T(8,128)(2,1)} %reshape.445, f32[2,6,256,256]{2,3,1,0:T(8,128)} %fusion.91, f32[2,6,256,256]{2,3,1,0:T(8,128)} %get-tuple-element.28, f32[2,6,256]{2,1,0:T(8,128)} %get-tuple-element.27), kind=kOutput, calls=%fused_computation.49 | convolution fusion | flops 106368256 | bytes 7090176 | tf_op jit(solution)/shard_map/bhqk,bkhd->bqhd/dot_general | solution.py:64
  261.8 5.1 all-to-all-start.9
  267.0 6.6 %fusion.46 = bf16[2,6,64,256]{3,2,1,0:T(8,128)(2,1)} fusion(bf16[2,256,6,64]{1,3,2,0:T(8,128)(2,1)} %reshape.444, f32[2,6,256,256]{2,3,1,0:T(8,128)} %fusion.91, f32[2,6,256,256]{2,3,1,0:T(8,128)} %get-tuple-element.28, f32[2,6,256]{2,1,0:T(8,128)} %get-tuple-element.27), kind=kOutput, calls=%fused_computation.50 | convolution fusion | flops 106368256 | bytes 7090176 | tf_op jit(solution)/shard_map/bhqk,bqhd->bkhd/dot_general | solution.py:70
  275.5 5.1 all-to-all-start.12
  306.4 5.8 %all-to-all-start.7 = ((bf16[1,64,1,8,384]{4,3,2,0,1:T(8,128)(2,1)}), bf16[1,64,1,8,384]{4,3,2,0,1:T(8,128)(2,1)S(1)}, u32[]{:S(2)}, u32[]{:S(2)}) async-start(bf16[1,64,1,8,384]{4,3,2,0,1:T(8,128)(2,1)} %copy.229), calls=%async_computation.7 | async-start | bytes 786432 | tf_op jit(solution)/shard_map/all_to_all | solution.py:233
  315.6 5.6 %all-to-all-done.7 = bf16[1,64,1,8,384]{4,3,2,0,1:T(8,128)(2,1)S(1)} async-done(((bf16[1,64,1,8,384]{4,3,2,0,1:T(8,128)(2,1)}), bf16[1,64,1,8,384]{4,3,2,0,1:T(8,128)(2,1)S(1)}, u32[]{:S(2)}, u32[]{:S(2)}) %all-to-all-start.7) | async-done | bytes 393248 | tf_op jit(solution)/shard_map/all_to_all | solution.py:233
  326.5 7.4 %all-to-all-done.3 = bf16[1,2,256,384]{3,1,0,2:T(2,128)(2,1)S(1)} async-done(((bf16[1,2,256,384]{3,1,0,2:T(2,128)(2,1)}), bf16[1,2,256,384]{3,1,0,2:T(2,128)(2,1)S(1)}, u32[]{:S(2)}, u32[]{:S(2)}) %all-to-all-start.3) | async-done | bytes 393248 | tf_op jit(solution)/shard_map/all_to_all | solution.py:211
  347.3 5.4 bitcast_convert_fusion
  354.7 9.3 %all-reduce = bf16[768]{0:T(1024)(128)(2,1)S(1)} all-reduce(bf16[768]{0:T(1024)(128)(2,1)S(1)} %get-tuple-element.7), channel_id=5, replica_groups=mesh['dp'=4,'fy'=4,'fx'=8] {'dp'}, use_global_device_ids=true, to_apply=%region_19.20.clone | all-reduce | flops 768 | bytes 3072
  364.1 64.7 %psum.50 = bf16[192]{0:T(256)(128)(2,1)S(1)} all-reduce(bf16[192]{0:T(256)(128)(2,1)S(1)} %dynamic-slice.1), channel_id=1, replica_groups=mesh['dp'=4,'fy'=4,'fx'=8] {'fy','fx'}, use_global_device_ids=true, to_apply=%region_18.19 | all-reduce | flops 192 | bytes 768 | tf_op jit(solution)/shard_map/psum | solution.py:341
  435.0 10.8 %psum.46 = f32[3,768]{1,0:T(4,128)S(1)} all-reduce(f32[3,768]{1,0:T(4,128)S(1)} %multiply_reduce_fusion.4), channel_id=1, replica_groups=mesh['dp'=4,'fy'=4,'fx'=8] {'dp'}, use_global_device_ids=true, to_apply=%region_21.22 | all-reduce | flops 2304 | bytes 18432 | tf_op jit(solution)/shard_map/psum | solution.py:336
  445.8 23.7 %psum.47 = f32[3,768]{1,0:T(4,128)S(1)} all-reduce(f32[3,768]{1,0:T(4,128)S(1)} %psum.46), channel_id=1, replica_groups=mesh['dp'=4,'fy'=4,'fx'=8] {'fx'}, use_global_device_ids=true, to_apply=%region_22.23 | all-reduce | flops 2304 | bytes 18432 | tf_op jit(solution)/shard_map/psum | solution.py:337
  470.1 70.0 %all-reduce.7.cloned.1.call-done = (bf16[192,2304]{1,0:T(8,128)(2,1)}, bf16[192,768]{1,0:T(8,128)(2,1)}) async-done(((bf16[192,2304]{1,0:T(8,128)(2,1)}, bf16[192,768]{1,0:T(8,128)(2,1)}), (bf16[192,2304]{1,0:T(8,128)(2,1)}, bf16[192,768]{1,0:T(8,128)(2,1)})) %all-reduce.7.cloned.1.call-update) | async-done | bytes 1179664 | tf_op jit(solution)/shard_map/psum | solution.py:339
  (194 shorter events, 199.0 us)
Async XLA Ops:
  8.0 55.0 %copy-start = (bf16[768,2304]{1,0:T(8,128)(2,1)S(1)}, bf16[768,2304]{1,0:T(8,128)(2,1)}, u32[]{:S(2)}) copy-start(bf16[768,2304]{1,0:T(8,128)(2,1)} %param.15) | copy-start | bytes 10616836
  10.5 8.9 %copy-start.27 = (s32[1,64]{1,0:T(1,128)S(1)}, s32[1,64]{1,0:T(1,128)}, u32[]{:S(2)}) copy-start(s32[1,64]{1,0:T(1,128)} %param.12) | copy-start | bytes 772
  12.2 54.9 %all-to-all-start.10 = ((bf16[1,16,4,8,384]{4,3,1,0,2:T(8,128)(2,1)}), bf16[1,16,4,8,384]{4,3,1,0,2:T(8,128)(2,1)}, u32[]{:S(2)}, u32[]{:S(2)}) async-start(bf16[1,16,4,8,384]{4,3,1,0,2:T(8,128)(2,1)} %copy.239), calls=%async_computation.10 | async-start | bytes 786432 | tf_op jit(solution)/shard_map/all_to_all | solution.py:273
  67.1 18.8 %all-to-all-start.6 = ((bf16[1,16,4,8,384]{4,3,1,0,2:T(8,128)(2,1)}), bf16[1,16,4,8,384]{4,3,1,0,2:T(8,128)(2,1)}, u32[]{:S(2)}, u32[]{:S(2)}) async-start(bf16[1,16,4,8,384]{4,3,1,0,2:T(8,128)(2,1)} %copy.224), calls=%async_computation.6 | async-start | bytes 786432 | tf_op jit(solution)/shard_map/all_to_all | solution.py:218
  85.9 13.1 %all-to-all-start.5 = ((bf16[1,16,4,8,384]{4,3,1,0,2:T(8,128)(2,1)}), bf16[1,16,4,8,384]{4,3,1,0,2:T(8,128)(2,1)}, u32[]{:S(2)}, u32[]{:S(2)}) async-start(bf16[1,16,4,8,384]{4,3,1,0,2:T(8,128)(2,1)} %copy.223), calls=%async_computation.5 | async-start | bytes 786432 | tf_op jit(solution)/shard_map/all_to_all | solution.py:215
  99.0 25.0 %copy-start.14 = (bf16[1,16,32,384]{3,2,1,0:T(8,128)(2,1)S(1)}, bf16[1,16,32,384]{3,2,1,0:T(8,128)(2,1)}, u32[]{:S(2)}) copy-start(bf16[1,16,32,384]{3,2,1,0:T(8,128)(2,1)} %get-tuple-element.15) | copy-start | bytes 1179652
  134.2 25.2 %all-to-all-start.1 = ((bf16[8,2,32,384]{3,2,1,0:T(8,128)(2,1)}), bf16[8,2,32,384]{3,2,1,0:T(8,128)(2,1)}, u32[]{:S(2)}, u32[]{:S(2)}) async-start(bf16[8,2,32,384]{3,2,1,0:T(8,128)(2,1)} %bitcast.250), calls=%async_computation.1 | async-start | bytes 786432 | tf_op jit(solution)/shard_map/all_to_all | solution.py:193
  159.4 16.3 %all-to-all-start = ((bf16[8,2,32,384]{3,2,1,0:T(8,128)(2,1)}), bf16[8,2,32,384]{3,2,1,0:T(8,128)(2,1)}, u32[]{:S(2)}, u32[]{:S(2)}) async-start(bf16[8,2,32,384]{3,2,1,0:T(8,128)(2,1)} %bitcast.249), calls=%async_computation | async-start | bytes 786432 | tf_op jit(solution)/shard_map/all_to_all | solution.py:199
  175.7 42.6 %all-to-all-start.11 = ((bf16[1,64,1,8,384]{4,3,2,0,1:T(8,128)(2,1)}), bf16[1,64,1,8,384]{4,3,2,0,1:T(8,128)(2,1)}, u32[]{:S(2)}, u32[]{:S(2)}) async-start(bf16[1,64,1,8,384]{4,3,2,0,1:T(8,128)(2,1)} %copy.244), calls=%async_computation.11 | async-start | bytes 786432 | tf_op jit(solution)/shard_map/all_to_all | solution.py:291
  218.3 12.9 %all-to-all-start.13 = ((bf16[1,64,1,8,384]{4,3,2,0,1:T(8,128)(2,1)}), bf16[1,64,1,8,384]{4,3,2,0,1:T(8,128)(2,1)}, u32[]{:S(2)}, u32[]{:S(2)}) async-start(bf16[1,64,1,8,384]{4,3,2,0,1:T(8,128)(2,1)} %copy.253), calls=%async_computation.13 | async-start | bytes 786432 | tf_op jit(solution)/shard_map/all_to_all | solution.py:292
  231.2 13.1 %all-to-all-start.15 = ((bf16[1,64,1,8,384]{4,3,2,0,1:T(8,128)(2,1)}), bf16[1,64,1,8,384]{4,3,2,0,1:T(8,128)(2,1)}, u32[]{:S(2)}, u32[]{:S(2)}) async-start(bf16[1,64,1,8,384]{4,3,2,0,1:T(8,128)(2,1)} %copy.262), calls=%async_computation.15 | async-start | bytes 786432 | tf_op jit(solution)/shard_map/all_to_all | solution.py:293
  244.3 17.6 %all-to-all-start.14 = ((bf16[1,2,256,384]{3,1,0,2:T(2,128)(2,1)}), bf16[1,2,256,384]{3,1,0,2:T(2,128)(2,1)}, u32[]{:S(2)}, u32[]{:S(2)}) async-start(bf16[1,2,256,384]{3,1,0,2:T(2,128)(2,1)} %copy.257), calls=%async_computation.14 | async-start | bytes 786432 | tf_op jit(solution)/shard_map/all_to_all | solution.py:262
  261.8 13.7 %all-to-all-start.9 = ((bf16[1,2,256,384]{3,1,0,2:T(2,128)(2,1)}), bf16[1,2,256,384]{3,1,0,2:T(2,128)(2,1)}, u32[]{:S(2)}, u32[]{:S(2)}) async-start(bf16[1,2,256,384]{3,1,0,2:T(2,128)(2,1)} %copy.236), calls=%async_computation.9 | async-start | bytes 786432 | tf_op jit(solution)/shard_map/all_to_all | solution.py:260
  275.5 16.3 %all-to-all-start.12 = ((bf16[1,2,256,384]{3,1,0,2:T(2,128)(2,1)}), bf16[1,2,256,384]{3,1,0,2:T(2,128)(2,1)}, u32[]{:S(2)}, u32[]{:S(2)}) async-start(bf16[1,2,256,384]{3,1,0,2:T(2,128)(2,1)} %copy.248), calls=%async_computation.12 | async-start | bytes 786432 | tf_op jit(solution)/shard_map/all_to_all | solution.py:261
  280.6 58.3 %reduce-scatter.4.cloned.1.call-start = ((), (), s32[]{:S(2)}) async-start(), calls=%async_computation.19 | async-start | bytes 884736 | tf_op jit(solution)/shard_map/reduce_scatter | solution.py:330
  306.4 14.9 %all-to-all-start.7 = ((bf16[1,64,1,8,384]{4,3,2,0,1:T(8,128)(2,1)}), bf16[1,64,1,8,384]{4,3,2,0,1:T(8,128)(2,1)S(1)}, u32[]{:S(2)}, u32[]{:S(2)}) async-start(bf16[1,64,1,8,384]{4,3,2,0,1:T(8,128)(2,1)} %copy.229), calls=%async_computation.7 | async-start | bytes 786432 | tf_op jit(solution)/shard_map/all_to_all | solution.py:233
  315.6 18.3 %copy-start.20 = (bf16[1,16,32,768]{3,2,1,0:T(8,128)(2,1)S(1)}, bf16[1,16,32,768]{3,2,1,0:T(8,128)(2,1)}, u32[]{:S(2)}) copy-start(bf16[1,16,32,768]{3,2,1,0:T(8,128)(2,1)} %param.17) | copy-start | bytes 2359300
  321.3 12.6 %all-to-all-start.3 = ((bf16[1,2,256,384]{3,1,0,2:T(2,128)(2,1)}), bf16[1,2,256,384]{3,1,0,2:T(2,128)(2,1)S(1)}, u32[]{:S(2)}, u32[]{:S(2)}) async-start(bf16[1,2,256,384]{3,1,0,2:T(2,128)(2,1)} %copy.219), calls=%async_computation.3 | async-start | bytes 786432 | tf_op jit(solution)/shard_map/all_to_all | solution.py:211
  326.4 105.9 %all-reduce.5.cloned.1.call-start = ((), (), s32[]{:S(2)}) async-start(), calls=%async_computation.20 | async-start | bytes 196608 | tf_op jit(solution)/shard_map/psum | solution.py:333
  338.9 95.0 %reduce-scatter.8.cloned.1.call-start = ((), (), s32[]{:S(2)}) async-start(), calls=%async_computation.22 | async-start | bytes 1474560 | tf_op jit(solution)/shard_map/reduce_scatter | solution.py:347
  339.8 94.0 %reduce-scatter.6.cloned.1.call-start = ((), (), s32[]{:S(2)}) async-start(), calls=%async_computation.21 | async-start | bytes 4423680 | tf_op jit(solution)/shard_map/reduce_scatter | solution.py:344
  352.8 76.6 %copy-start.3 = (f32[1,16,32,768]{3,2,1,0:T(8,128)S(1)}, f32[1,16,32,768]{3,2,1,0:T(8,128)}, u32[]{:S(2)}) copy-start(f32[1,16,32,768]{3,2,1,0:T(8,128)} %broadcast_in_dim.39) | copy-start | bytes 4718596
  352.8 76.6 %copy-start.13 = (bf16[1,16,32,768]{3,2,1,0:T(8,128)(2,1)S(1)}, bf16[1,16,32,768]{3,2,1,0:T(8,128)(2,1)}, u32[]{:S(2)}) copy-start(bf16[1,16,32,768]{3,2,1,0:T(8,128)(2,1)} %param.9) | copy-start | bytes 2359300
  352.8 187.4 %all-reduce.7.cloned.1.call-start = ((), (), s32[]{:S(2)}) async-start(), calls=%async_computation.23 | async-start | bytes 2359296 | tf_op jit(solution)/shard_map/psum | solution.py:339
  (24 other events, 73.0 us)
Sparse Core Ops, SparseCore 0:
  302.8 36.0 reduce-scatter.3
  341.4 45.4 all-reduce.4
Sparse Core Ops, SparseCore 1:
  342.4 26.8 reduce-scatter.7
  371.5 42.9 reduce-scatter.5
  434.0 106.1 all-reduce.6
